TPU v7x, 32 devices: a whole 2x2x4 slice. The times are simulated.
32 devices in a mesh: ctx: 4 (over y, x), exp: 8 (over z, core).
Axes of the slice: x: 2, y: 2, z: 4, core: 2. Of those that a mesh axis runs over, the one named last changes fastest.
Arguments:
- residual: bfloat16 [512, 4096], P('ctx'), may hold values from -4 to 4
- ssm_input: bfloat16 [512, 8192], P('ctx', 'exp'), may hold values from -16 to 16
- ssm_gate: bfloat16 [512, 8192], P('ctx', 'exp'), may hold values from -5 to 5
- write_vectors: bfloat16 [512, 128], P('ctx'), may hold values from -1.75 to 1.75
- read_vectors: bfloat16 [512, 128], P('ctx'), may hold values from -1.75 to 1.75
- step_logits: float32 [128, 512], P('exp', 'ctx'), may hold values from -2 to 1536
- decay_log: float32 [128], P('exp'), may hold values from -12 to -2
- skip_gain: float32 [128], P('exp'), may hold values from 0.5 to 3
- norm_gain: float32 [8192], P('exp'), may hold values from 0.1 to 1.9
- out_weight: bfloat16 [8192, 4096], P('exp', 'ctx'), may hold values from -0.09375 to 0.09375
- moe_gain: float32 [4096], replicated, may hold values from 0.1 to 1.9
- gate_weight: bfloat16 [8, 4096, 12288], P('exp', None, 'ctx'), may hold values from -0.09375 to 0.09375
- up_weight: bfloat16 [8, 4096, 12288], P('exp', None, 'ctx'), may hold values from -0.09375 to 0.09375
- down_weight: bfloat16 [8, 12288, 4096], P('exp', 'ctx'), may hold values from -0.0546875 to 0.0546875
- expert_ids: int32 [512, 2], P('ctx'), may hold values from 0 to 7, all different within a row; in each aligned block of 128 rows (0 to 127, 128 to 255, ...) at most 64 rows name the same one
- route_weight: float32 [512, 2], P('ctx'), may hold values from 0.5 to 1.5
Outputs:
- layer_out: bfloat16 [512, 4096], P('ctx', 'exp')
Inputs may be any that keep to these rules, and one draw needn't show every extreme that they name: `expert_ids`: each row names 2 different experts. Among the 128 rows of one index of ctx no expert is named by more than 64 rows, and in every draw some expert is named by exactly 64 of them.
All inputs are finite; a program needn't handle non-finite values.
Results may differ from a plain program's by a relative error of at most 0.023.
Values may be sent and summed in bfloat16 or wider, within the bound.
A program may use at most 192 MiB of HBM per device.

v0:
```python
import jax
import jax.numpy as jnp
from jax import lax
from jax.sharding import PartitionSpec as P

SPAN = 128
NORM_GROUP = 512
EXPERTS = 8
CAP = 64


EPSILON = 1e-05


def passed_along(block, axis, distance):
    devices = range(lax.axis_size(axis))
    route = [(i - distance, i) for i in devices if i - distance in devices]
    return lax.ppermute(block, axis, route)


def slot_tables(block_ids):
    expert_range = jnp.arange(EXPERTS, dtype=jnp.int32)
    hit_table = jnp.sum(
        (block_ids[:, :, None] == expert_range[None, None, :]).astype(jnp.int32), axis=1
    )
    ranking = jnp.cumsum(hit_table, axis=0) - 1
    slot_range = jnp.arange(CAP, dtype=jnp.int32)
    matches = (hit_table.T[:, None, :] == 1) & (ranking.T[:, None, :] == slot_range[None, :, None])
    row_count = block_ids.shape[0]
    row_range = jnp.arange(row_count, dtype=jnp.int32)
    chosen = jnp.sum(jnp.where(matches, row_range[None, None, :], 0), axis=2)
    filled = jnp.any(matches, axis=2)
    token_of_slot = jnp.where(filled, chosen, row_count)
    pick_rank = jnp.take_along_axis(ranking, block_ids, axis=1)
    return (token_of_slot, pick_rank)


def normalize(stream_rows, moe_gain):
    values = stream_rows.astype(jnp.float32)
    scale_inv = lax.rsqrt(jnp.mean(values * values, axis=-1, keepdims=True) + EPSILON)
    return (values * scale_inv * moe_gain).astype(jnp.bfloat16)


def body(
    residual,
    ssm_input,
    ssm_gate,
    write_vectors,
    read_vectors,
    step_logits,
    decay_log,
    skip_gain,
    norm_gain,
    out_weight,
    moe_gain,
    gate_weight,
    up_weight,
    down_weight,
    expert_ids,
    route_weight,
):
    heads_dev = step_logits.shape[0]
    tok_rows = step_logits.shape[1]
    head_width = ssm_input.shape[1] // heads_dev
    span_count = tok_rows // SPAN
    step_size = jax.nn.softplus(step_logits)
    log_step = step_size * (-jnp.exp(decay_log))[:, None]
    cumulative = jnp.cumsum(log_step.reshape(heads_dev, span_count, SPAN), axis=2)
    step_blocks = step_size.reshape(heads_dev, span_count, SPAN)
    input_blocks = ssm_input.reshape(span_count, SPAN, heads_dev, head_width)
    write_blocks = write_vectors.reshape(span_count, SPAN, -1)
    read_blocks = read_vectors.reshape(span_count, SPAN, -1)
    scores = jnp.einsum(
        "ktn,ksn->kts", read_blocks, write_blocks, preferred_element_type=jnp.float32
    )
    causal = jnp.arange(SPAN)[:, None] >= jnp.arange(SPAN)[None, :]
    log_gaps = cumulative[:, :, :, None] - cumulative[:, :, None, :]
    mixing = jnp.where(
        causal,
        scores[None] * jnp.exp(jnp.where(causal, log_gaps, 0.0)) * step_blocks[:, :, None, :],
        0.0,
    ).astype(jnp.bfloat16)
    intra_out = jnp.einsum(
        "hkts,kshp->kthp", mixing, input_blocks, preferred_element_type=jnp.float32
    )
    end_weight = jnp.exp(cumulative[:, :, -1:] - cumulative) * step_blocks
    loaded = (end_weight[:, :, :, None] * write_blocks.astype(jnp.float32)[None]).astype(
        jnp.bfloat16
    )
    block_state = jnp.einsum(
        "kshp,hksn->hkpn", input_blocks, loaded, preferred_element_type=jnp.float32
    )
    block_decay = jnp.exp(cumulative[:, :, -1])
    running = jnp.zeros_like(block_state[:, 0])
    decay_run = jnp.ones_like(block_decay[:, 0])
    entering_list = [running]
    reach_list = [decay_run]
    running = block_decay[:, 0, None, None] * running + block_state[:, 0]
    decay_run = decay_run * block_decay[:, 0]
    device_state = running
    device_decay = decay_run

    def forward(turn_index, incoming):
        return passed_along(
            (device_decay[:, None, None] * incoming + device_state).astype(jnp.bfloat16), "ctx", 1
        ).astype(jnp.float32)

    device_in = lax.fori_loop(0, lax.axis_size("ctx") - 1, forward, jnp.zeros_like(device_state))
    entering = jnp.stack(entering_list, axis=1)
    reach = jnp.stack(reach_list, axis=1)
    states = entering + reach[:, :, None, None] * device_in[:, None]
    inter_out = jnp.transpose(jnp.exp(cumulative), (1, 2, 0))[:, :, :, None] * jnp.einsum(
        "ktn,hkpn->kthp", read_blocks.astype(jnp.float32), states, precision=lax.Precision.HIGHEST
    )
    scan_out = (
        intra_out + inter_out + skip_gain[None, None, :, None] * input_blocks.astype(jnp.float32)
    )
    scan_out = scan_out.reshape(tok_rows, heads_dev * head_width)
    gated_out = scan_out * jax.nn.silu(ssm_gate.astype(jnp.float32))
    grouped = gated_out.reshape(tok_rows, -1, NORM_GROUP)
    group_scale = lax.rsqrt(jnp.mean(grouped * grouped, axis=2, keepdims=True) + EPSILON)
    normed = ((grouped * group_scale).reshape(tok_rows, -1) * norm_gain).astype(jnp.bfloat16)
    ssm_terms = jnp.dot(
        normed,
        lax.all_gather(out_weight, "ctx", axis=1, tiled=True),
        preferred_element_type=jnp.float32,
    )
    exp_count = lax.axis_size("exp")
    exp_index = lax.axis_index("exp")
    slice_width = residual.shape[1] // exp_count
    split_count = exp_count // EXPERTS
    own_residual = lax.dynamic_slice_in_dim(residual, exp_index * slice_width, slice_width, 1)
    ssm_sum = lax.psum(ssm_terms.astype(jnp.bfloat16), "exp").astype(jnp.float32)
    ssm_share = lax.dynamic_slice_in_dim(ssm_sum, exp_index * slice_width, slice_width, 1)
    stream_slice = (own_residual.astype(jnp.float32) + ssm_share).astype(jnp.bfloat16)
    token_of_slot, pick_rank = slot_tables(expert_ids)
    stream_full = lax.all_gather(stream_slice, "exp", axis=1, tiled=True)
    padded = jnp.concatenate(
        [stream_full, jnp.zeros((1, stream_full.shape[1]), jnp.bfloat16)], axis=0
    )
    my_slots = lax.dynamic_index_in_dim(token_of_slot, exp_index // split_count, 0, keepdims=False)
    picked = normalize(jnp.take(padded, my_slots, axis=0), moe_gain)
    normed_rows = lax.all_gather(picked, "ctx", axis=0, tiled=True)
    gate_val = jnp.dot(normed_rows, gate_weight[0], preferred_element_type=jnp.float32)
    up_val = jnp.dot(normed_rows, up_weight[0], preferred_element_type=jnp.float32)
    hidden = (jax.nn.silu(gate_val) * up_val).astype(jnp.bfloat16)
    sums_mine = lax.psum_scatter(
        jnp.dot(hidden, down_weight[0], preferred_element_type=jnp.float32).astype(jnp.bfloat16),
        "ctx",
        scatter_dimension=0,
        tiled=True,
    ).astype(jnp.float32)
    arrived = lax.all_to_all(
        sums_mine.astype(jnp.bfloat16), "exp", split_axis=1, concat_axis=0, tiled=True
    ).astype(sums_mine.dtype)
    piece_expert = jnp.arange(exp_count, dtype=jnp.int32) // split_count
    hit_expert = (expert_ids[:, :, None] == piece_expert[None, None, :]).astype(jnp.float32)
    hit_slot = (pick_rank[:, :, None] == jnp.arange(CAP, dtype=jnp.int32)[None, None, :]).astype(
        jnp.float32
    )
    combine_table = jnp.sum(
        route_weight[:, :, None, None] * hit_expert[:, :, :, None] * hit_slot[:, :, None, :], axis=1
    )
    combine_table = combine_table.reshape(tok_rows, exp_count * CAP)
    moe_slice = jnp.dot(
        combine_table, arrived, precision=lax.Precision.HIGHEST, preferred_element_type=jnp.float32
    )
    return (stream_slice.astype(jnp.float32) + moe_slice).astype(jnp.bfloat16)


def solution(mesh):
    placed = (
        P("ctx", None),
        P("ctx", "exp"),
        P("ctx", "exp"),
        P("ctx", None),
        P("ctx", None),
        P("exp", "ctx"),
        P("exp"),
        P("exp"),
        P("exp"),
        P("exp", "ctx"),
        P(),
        P("exp", None, "ctx"),
        P("exp", None, "ctx"),
        P("exp", "ctx", None),
        P("ctx", None),
        P("ctx", None),
    )
    return jax.shard_map(
        body, mesh=mesh, in_specs=placed, out_specs=P("ctx", "exp"), check_vma=False
    )
```

profile of v0, /device:TPU:0, one launch (start us, length us, event | category | flops | bytes accessed | tf_op | source)
XLA Modules:
  0.0 343.4 jit_solution(16639426668395161547)
XLA Ops:
  6.6 0.7 all-gather.4.cloned.1.call-update
  7.3 1.1 copy.60
  8.5 1.1 copy.61
  10.3 0.5 fusion.27
  10.9 42.7 %while.11 = (s32[]{:T(128)}, f32[16,64,128]{2,1,0:T(8,128)S(1)}, f32[16,1]{0,1:T(1,128)S(1)}, f32[16,64,128]{2,1,0:T(8,128)S(1)}, s32[]{:T(128)}, /*index=5*/s32[]{:T(128)}) while((s32[]{:T(128)}, f32[16,64,128]{2,1,0:T(8,128)S(1)}, f32[16,1]{0,1:T(1,128)S(1)}, f32[16,64,128]{2,1,0:T(8,128)S(1)}, s32[]{:T(128)}, ...), condition=%wide.region_2.3_spmd.clone, body=%wide.region_1.2_spmd.clone.sunk | while | flops 655363 | bytes 3145911 | solution.py:108
  11.0 4.9 %collective-permute-start = (bf16[16,64,128]{2,1,0:T(8,128)(2,1)S(1)}, bf16[16,64,128]{2,1,0:T(8,128)(2,1)S(1)}, u32[]{:S(2)}, u32[]{:S(2)}) collective-permute-start(bf16[16,64,128]{2,1,0:T(8,128)(2,1)S(1)} %fusion.72), channel_id=1, source_target_pairs={{0,8},{8,16},{16,24},{1,9},{9,17},{17,25},{2,10},{10,18},{18,26},{... | collective-permute-start | bytes 786440 | tf_op jit(solution)/shard_map/while/body/eval_jaxpr/ppermute | solution.py:18
  15.9 5.5 %collective-permute-done = bf16[16,64,128]{2,1,0:T(8,128)(2,1)S(1)} collective-permute-done((bf16[16,64,128]{2,1,0:T(8,128)(2,1)S(1)}, bf16[16,64,128]{2,1,0:T(8,128)(2,1)S(1)}, u32[]{:S(2)}, u32[]{:S(2)}) %collective-permute-start) | collective-permute-done | bytes 262176 | tf_op jit(solution)/shard_map/while/body/eval_jaxpr/ppermute | solution.py:18
  21.6 4.4 %collective-permute-start = (bf16[16,64,128]{2,1,0:T(8,128)(2,1)S(1)}, bf16[16,64,128]{2,1,0:T(8,128)(2,1)S(1)}, u32[]{:S(2)}, u32[]{:S(2)}) collective-permute-start(bf16[16,64,128]{2,1,0:T(8,128)(2,1)S(1)} %fusion.72), channel_id=1, source_target_pairs={{0,8},{8,16},{16,24},{1,9},{9,17},{17,25},{2,10},{10,18},{18,26},{... | collective-permute-start | bytes 786440 | tf_op jit(solution)/shard_map/while/body/eval_jaxpr/ppermute | solution.py:18
  26.0 11.6 %collective-permute-done = bf16[16,64,128]{2,1,0:T(8,128)(2,1)S(1)} collective-permute-done((bf16[16,64,128]{2,1,0:T(8,128)(2,1)S(1)}, bf16[16,64,128]{2,1,0:T(8,128)(2,1)S(1)}, u32[]{:S(2)}, u32[]{:S(2)}) %collective-permute-start) | collective-permute-done | bytes 262176 | tf_op jit(solution)/shard_map/while/body/eval_jaxpr/ppermute | solution.py:18
  37.8 4.4 %collective-permute-start = (bf16[16,64,128]{2,1,0:T(8,128)(2,1)S(1)}, bf16[16,64,128]{2,1,0:T(8,128)(2,1)S(1)}, u32[]{:S(2)}, u32[]{:S(2)}) collective-permute-start(bf16[16,64,128]{2,1,0:T(8,128)(2,1)S(1)} %fusion.72), channel_id=1, source_target_pairs={{0,8},{8,16},{16,24},{1,9},{9,17},{17,25},{2,10},{10,18},{18,26},{... | collective-permute-start | bytes 786440 | tf_op jit(solution)/shard_map/while/body/eval_jaxpr/ppermute | solution.py:18
  42.2 11.3 %collective-permute-done = bf16[16,64,128]{2,1,0:T(8,128)(2,1)S(1)} collective-permute-done((bf16[16,64,128]{2,1,0:T(8,128)(2,1)S(1)}, bf16[16,64,128]{2,1,0:T(8,128)(2,1)S(1)}, u32[]{:S(2)}, u32[]{:S(2)}) %collective-permute-start) | collective-permute-done | bytes 262176 | tf_op jit(solution)/shard_map/while/body/eval_jaxpr/ppermute | solution.py:18
  53.6 0.4 fusion.26
  54.1 0.6 fusion.29
  55.1 0.4 mul.209
  56.1 54.2 %all-gather.4.cloned.1.call-done = bf16[1024,4096]{1,0:T(8,128)(2,1)} async-done(((bf16[1024,1024]{1,0:T(8,128)(2,1)}), bf16[1024,4096]{1,0:T(8,128)(2,1)}) %all-gather.4.cloned.1.call-update) | async-done | bytes 8388624 | tf_op jit(solution)/shard_map/all_gather | solution.py:125
  110.3 5.8 %convolution_convert_fusion = bf16[128,4096]{1,0:T(8,128)(2,1)} fusion(bf16[1024,4096]{1,0:T(8,128)(2,1)} %all-gather.4.cloned.1.call-done, f32[128,1024]{1,0:T(8,128)S(1)} %bitcast.99, f32[1024]{0:T(1024)S(1)} %copy-done.10, f32[128,1024]{1,0:T(8,128)S(1)} %copy.62, bf16[128,1024]{1,0:T(8,128)(2,1)S(1)} %copy-done.3), kind=kOutput, calls=%fused_computation.12 | convolution fusion | flops 1075445760 | bytes 10752000 | tf_op jit(solution)/shard_map/dot_general | solution.py:123
  116.2 58.9 %all-reduce.3.cloned.1.call-done = bf16[128,4096]{1,0:T(8,128)(2,1)} async-done(((bf16[128,4096]{1,0:T(8,128)(2,1)}), bf16[128,4096]{1,0:T(8,128)(2,1)}) %all-reduce.3.cloned.1.call-update) | async-done | bytes 1048592 | tf_op jit(solution)/shard_map/psum | solution.py:133
  175.1 1.7 add_convert_fusion
  177.8 20.3 %all-gather.6.cloned.1.call-done = bf16[128,4096]{1,0:T(8,128)(2,1)} async-done(((bf16[128,512]{1,0:T(8,128)(2,1)}), bf16[128,4096]{1,0:T(8,128)(2,1)}) %all-gather.6.cloned.1.call-update) | async-done | bytes 1048592 | tf_op jit(solution)/shard_map/all_gather | solution.py:137
  198.0 1.3 concatenate.3
  199.4 0.9 gather_fusion
  200.2 0.3 fusion.32
  200.6 1.0 fusion.34
  201.8 34.9 %all-gather.8.cloned.1.call-done = bf16[256,4096]{1,0:T(8,128)(2,1)} async-done(((bf16[64,4096]{1,0:T(8,128)(2,1)}), bf16[256,4096]{1,0:T(8,128)(2,1)}) %all-gather.8.cloned.1.call-update) | async-done | bytes 2097168 | tf_op jit(solution)/shard_map/all_gather | solution.py:143
  236.7 16.7 %fusion.6 = f32[256,3072]{1,0:T(8,128)} fusion(bf16[256,4096]{1,0:T(8,128)(2,1)} %all-gather.8.cloned.1.call-done, bf16[1,4096,3072]{2,1,0:T(8,128)(2,1)} %param.29), kind=kOutput, calls=%fused_computation.9 | convolution fusion | flops 6442450944 | bytes 30408704 | tf_op jit(solution)/shard_map/dot_general | solution.py:144
  253.4 25.1 %fusion.8 = bf16[256,4096]{1,0:T(8,128)(2,1)} fusion(bf16[1,3072,4096]{2,1,0:T(8,128)(2,1)} %param.31, bf16[256,4096]{1,0:T(8,128)(2,1)S(1)} %copy-done.9, bf16[1,4096,3072]{2,1,0:T(8,128)(2,1)} %param.30, f32[256,3072]{1,0:T(8,128)} %fusion.6), kind=kOutput, calls=%fused_computation.11 | convolution fusion | flops 12890669056 | bytes 57671680 | tf_op jit(solution)/shard_map/dot_general | solution.py:148
  278.5 35.4 %reduce-scatter.2.cloned.1.call-done = bf16[64,4096]{1,0:T(8,128)(2,1)} async-done(((bf16[256,4096]{1,0:T(8,128)(2,1)}), bf16[64,4096]{1,0:T(8,128)(2,1)}) %reduce-scatter.2.cloned.1.call-update) | async-done | bytes 524304 | tf_op jit(solution)/shard_map/reduce_scatter | solution.py:147
  313.9 1.9 copy.74
  315.8 4.6 %all-to-all-start = ((bf16[64,8,512]{2,0,1:T(8,128)(2,1)}), bf16[64,8,512]{2,0,1:T(8,128)(2,1)S(1)}, u32[]{:S(2)}, u32[]{:S(2)}) async-start(bf16[64,8,512]{2,0,1:T(8,128)(2,1)} %bitcast.90), calls=%async_computation.1 | async-start | bytes 1048576 | tf_op jit(solution)/shard_map/all_to_all | solution.py:153
  320.7 1.9 gather_fusion.1
  323.0 12.8 %all-to-all-done = bf16[64,8,512]{2,0,1:T(8,128)(2,1)S(1)} async-done(((bf16[64,8,512]{2,0,1:T(8,128)(2,1)}), bf16[64,8,512]{2,0,1:T(8,128)(2,1)S(1)}, u32[]{:S(2)}, u32[]{:S(2)}) %all-to-all-start) | async-done | bytes 524320 | tf_op jit(solution)/shard_map/all_to_all | solution.py:153
  335.8 1.1 fusion.31
  (79 shorter events, 4.1 us)
Async XLA Ops:
  6.5 47.1 %copy-start = (bf16[128,128]{1,0:T(8,128)(2,1)S(1)}, bf16[128,128]{1,0:T(8,128)(2,1)}, u32[]{:S(2)}) copy-start(bf16[128,128]{1,0:T(8,128)(2,1)} %param.22) | copy-start | bytes 98308
  6.5 3.0 copy-start.4
  6.5 3.0 copy-start.11
  6.5 3.1 copy-start.5
  6.5 103.8 %all-gather.4.cloned.1.call-start = ((), (), s32[]{:S(2)}) async-start(), calls=%async_computation.2 | async-start | bytes 10485760 | tf_op jit(solution)/shard_map/all_gather | solution.py:125
  7.3 167.9 %all-reduce.3.cloned.1.call-start = ((), (), s32[]{:S(2)}) async-start(), calls=%async_computation.3 | async-start | bytes 2097152 | tf_op jit(solution)/shard_map/psum | solution.py:133
  10.8 43.3 %copy-start.12 = (f32[16]{0:T(128)S(1)}, f32[16]{0:T(128)}, u32[]{:S(2)}) copy-start(f32[16]{0:T(128)} %param.25) | copy-start | bytes 196
  11.0 10.4 %collective-permute-start = (bf16[16,64,128]{2,1,0:T(8,128)(2,1)S(1)}, bf16[16,64,128]{2,1,0:T(8,128)(2,1)S(1)}, u32[]{:S(2)}, u32[]{:S(2)}) collective-permute-start(bf16[16,64,128]{2,1,0:T(8,128)(2,1)S(1)} %fusion.72), channel_id=1, source_target_pairs={{0,8},{8,16},{16,24},{1,9},{9,17},{17,25},{2,10},{10,18},{18,26},{... | collective-permute-start | bytes 786440 | tf_op jit(solution)/shard_map/while/body/eval_jaxpr/ppermute | solution.py:18
  21.6 16.0 %collective-permute-start = (bf16[16,64,128]{2,1,0:T(8,128)(2,1)S(1)}, bf16[16,64,128]{2,1,0:T(8,128)(2,1)S(1)}, u32[]{:S(2)}, u32[]{:S(2)}) collective-permute-start(bf16[16,64,128]{2,1,0:T(8,128)(2,1)S(1)} %fusion.72), channel_id=1, source_target_pairs={{0,8},{8,16},{16,24},{1,9},{9,17},{17,25},{2,10},{10,18},{18,26},{... | collective-permute-start | bytes 786440 | tf_op jit(solution)/shard_map/while/body/eval_jaxpr/ppermute | solution.py:18
  37.8 15.7 %collective-permute-start = (bf16[16,64,128]{2,1,0:T(8,128)(2,1)S(1)}, bf16[16,64,128]{2,1,0:T(8,128)(2,1)S(1)}, u32[]{:S(2)}, u32[]{:S(2)}) collective-permute-start(bf16[16,64,128]{2,1,0:T(8,128)(2,1)S(1)} %fusion.72), channel_id=1, source_target_pairs={{0,8},{8,16},{16,24},{1,9},{9,17},{17,25},{2,10},{10,18},{18,26},{... | collective-permute-start | bytes 786440 | tf_op jit(solution)/shard_map/while/body/eval_jaxpr/ppermute | solution.py:18
  53.6 1.3 copy-start.3
  54.7 55.6 %copy-start.10 = (f32[1024]{0:T(1024)S(1)}, f32[1024]{0:T(1024)}, u32[]{:S(2)}) copy-start(f32[1024]{0:T(1024)} %param.26) | copy-start | bytes 12292
  110.3 66.5 %copy-start.7 = (s32[128,2]{0,1:T(2,128)S(1)}, s32[128,2]{0,1:T(2,128)}, u32[]{:S(2)}) copy-start(s32[128,2]{0,1:T(2,128)} %param.32) | copy-start | bytes 3076
  116.2 81.8 %all-gather.6.cloned.1.call-start = ((), (), s32[]{:S(2)}) async-start(), calls=%async_computation.4 | async-start | bytes 1179648 | tf_op jit(solution)/shard_map/all_gather | solution.py:137
  176.8 59.9 %all-gather.8.cloned.1.call-start = ((), (), s32[]{:S(2)}) async-start(), calls=%async_computation.5 | async-start | bytes 2621440 | tf_op jit(solution)/shard_map/all_gather | solution.py:143
  199.4 1.2 copy-start.6
  201.6 112.3 %reduce-scatter.2.cloned.1.call-start = ((), (), s32[]{:S(2)}) async-start(), calls=%async_computation.6 | async-start | bytes 2621440 | tf_op jit(solution)/shard_map/reduce_scatter | solution.py:147
  236.7 16.7 %copy-start.9 = (bf16[256,4096]{1,0:T(8,128)(2,1)S(1)}, bf16[256,4096]{1,0:T(8,128)(2,1)}, u32[]{:S(2)}) copy-start(bf16[256,4096]{1,0:T(8,128)(2,1)} %all-gather.8.cloned.1.call-done) | copy-start | bytes 6291460
  315.8 20.0 %all-to-all-start = ((bf16[64,8,512]{2,0,1:T(8,128)(2,1)}), bf16[64,8,512]{2,0,1:T(8,128)(2,1)S(1)}, u32[]{:S(2)}, u32[]{:S(2)}) async-start(bf16[64,8,512]{2,0,1:T(8,128)(2,1)} %bitcast.90), calls=%async_computation.1 | async-start | bytes 1048576 | tf_op jit(solution)/shard_map/all_to_all | solution.py:153
  320.7 2.2 copy-start.8
  320.7 15.1 %copy-start.2 = (bf16[128,512]{1,0:T(8,128)(2,1)S(1)}, bf16[128,512]{1,0:T(8,128)(2,1)}, u32[]{:S(2)}) copy-start(bf16[128,512]{1,0:T(8,128)(2,1)} %add_convert_fusion) | copy-start | bytes 393220
  320.7 16.2 %copy-start.1 = (bf16[128,128]{1,0:T(8,128)(2,1)S(1)}, bf16[128,128]{1,0:T(8,128)(2,1)}, u32[]{:S(2)}) copy-start(bf16[128,128]{1,0:T(8,128)(2,1)} %param.22) | copy-start | bytes 98308
Sparse Core Ops, SparseCore 0:
  9.2 101.0 all-gather.3
  116.3 58.7 all-reduce.2
  176.9 21.0 all-gather.5
  201.7 34.9 all-gather.7
  278.7 35.1 reduce-scatter.1
where the time goes:
time: 344 us; the launch traced here: 343 us
  waiting for transfers between devices  246 us (72%)
  matrix products  50.4 us (15%)
  starting transfers between devices  18.6 us (5%)
  between operations  13.5 us (4%)
  local copies, waits for them, and re-layouts  9.85 us (3%)
  other arithmetic  5.34 us (2%)
    psum x1, waiting for transfers between devices, body(): lax.psum(ssm_terms.astype(jnp.bfloat16), 'exp').astype(jnp.float32)  58.9 us
    all_gather x1, waiting for transfers between devices, body(): lax.all_gather(out_weight, 'ctx', axis=1, tiled=True)  54.2 us
    reduce_scatter x1, waiting for transfers between devices, body(): lax.psum_scatter(jnp.dot(hidden, down_weight[0], preferred_element_type=j...  35.4 us
    all_gather x1, waiting for transfers between devices, body(): normed_rows = lax.all_gather(picked, 'ctx', axis=0, tiled=True)  34.9 us
    ppermute x3, waiting for transfers between devices, passed_along(): return lax.ppermute(block, axis, route)  28.4 us
    dot_general x1, matrix products, body(): jnp.dot(hidden, down_weight[0], preferred_element_type=jnp.float32)  25.1 us
    all_gather x1, waiting for transfers between devices, body(): stream_full = lax.all_gather(stream_slice, 'exp', axis=1, tiled=True)  20.3 us
    dot_general x1, matrix products, body(): jnp.dot(normed_rows, gate_weight[0], preferred_element_type=jnp.float32)  16.7 us
  transfers between devices with their start and end apart: 9, of which 9 were waited for; matrix products, arithmetic and copies ran while one was open for 3% of the time, Pallas kernels for 0%

commit v1 on v0

--- a/solution.py
+++ b/solution.py
@@ -1,6 +1,11 @@
+import functools
+import math
+
 import jax
 import jax.numpy as jnp
 from jax import lax
+from jax.experimental import pallas as pl
+from jax.experimental.pallas import tpu as pltpu
 from jax.sharding import PartitionSpec as P
 
 SPAN = 128
@@ -12,10 +17,181 @@
 EPSILON = 1e-05
 
 
-def passed_along(block, axis, distance):
-    devices = range(lax.axis_size(axis))
-    route = [(i - distance, i) for i in devices if i - distance in devices]
-    return lax.ppermute(block, axis, route)
+MESH = pl.DeviceIdType.MESH
+
+
+def send_kernel(axis, count, pair, spread, n_arrays, *refs):
+    sources, targets = refs[:n_arrays], refs[n_arrays : 2 * n_arrays]
+    local_sem, send_sem, recv_sem = refs[2 * n_arrays :]
+    index = lax.axis_index(axis)
+    group, lane = index // pair, lax.rem(index, pair)
+    barrier = pltpu.get_barrier_semaphore()
+    peers = [lax.rem(group + d, count) for d in range(1, count)]
+    for peer in peers:
+        pl.semaphore_signal(
+            barrier, inc=1, device_id={axis: peer * pair + lane}, device_id_type=MESH
+        )
+    pl.semaphore_wait(barrier, count - 1)
+    copies = []
+    for d, peer in enumerate(peers):
+        for i in range(n_arrays):
+            copy = pltpu.make_async_remote_copy(
+                src_ref=sources[i] if spread else sources[i].at[peer],
+                dst_ref=targets[i].at[group],
+                send_sem=send_sem.at[d, i],
+                recv_sem=recv_sem.at[d, i],
+                device_id={axis: peer * pair + lane},
+                device_id_type=MESH,
+            )
+            copy.start()
+            copies.append(copy)
+    for i in range(n_arrays):
+        own = pltpu.make_async_copy(
+            sources[i] if spread else sources[i].at[group],
+            targets[i].at[group],
+            local_sem.at[i],
+        )
+        own.start()
+        copies.append(own)
+    for copy in copies:
+        copy.wait()
+
+
+def sent(arrays, axis, number, spread, pair=1):
+    count = lax.axis_size(axis) // pair
+    n_arrays = len(arrays)
+    shapes = [
+        jax.ShapeDtypeStruct((count,) + a.shape if spread else a.shape, a.dtype) for a in arrays
+    ]
+    size = sum(math.prod(shape.shape) * shape.dtype.itemsize for shape in shapes)
+    return pl.pallas_call(
+        functools.partial(send_kernel, axis, count, pair, spread, n_arrays),
+        out_shape=shapes,
+        in_specs=[pl.BlockSpec(memory_space=pl.ANY)] * n_arrays,
+        out_specs=[pl.BlockSpec(memory_space=pl.ANY)] * n_arrays,
+        scratch_shapes=[
+            pltpu.SemaphoreType.DMA((n_arrays,)),
+            pltpu.SemaphoreType.DMA((count - 1, n_arrays)),
+            pltpu.SemaphoreType.DMA((count - 1, n_arrays)),
+        ],
+        compiler_params=pltpu.CompilerParams(collective_id=number, has_side_effects=True),
+        cost_estimate=pl.CostEstimate(flops=0, bytes_accessed=2 * size, transcendentals=0),
+    )(*arrays)
+
+
+def gather_pairs_kernel(axis, groups, x_ref, out_ref, local_sem, send_sem, recv_sem, pass_send, pass_recv):
+    index = lax.axis_index(axis)
+    group, lane = index // 2, lax.rem(index, 2)
+    sibling = group * 2 + 1 - lane
+    barrier = pltpu.get_barrier_semaphore()
+    peers = [lax.rem(group + d, groups) for d in range(1, groups)]
+    for peer in [p * 2 + lane for p in peers] + [sibling]:
+        pl.semaphore_signal(barrier, inc=1, device_id={axis: peer}, device_id_type=MESH)
+    pl.semaphore_wait(barrier, groups)
+    copies = []
+    for d, peer in enumerate(peers):
+        copy = pltpu.make_async_remote_copy(
+            src_ref=x_ref,
+            dst_ref=out_ref.at[index],
+            send_sem=send_sem.at[d],
+            recv_sem=recv_sem.at[d],
+            device_id={axis: peer * 2 + lane},
+            device_id_type=MESH,
+        )
+        copy.start()
+        copies.append(copy)
+    own = pltpu.make_async_copy(x_ref, out_ref.at[index], local_sem)
+    own.start()
+    passed = [
+        pltpu.make_async_remote_copy(
+            src_ref=x_ref,
+            dst_ref=out_ref.at[index],
+            send_sem=pass_send.at[0],
+            recv_sem=pass_recv.at[0],
+            device_id={axis: sibling},
+            device_id_type=MESH,
+        )
+    ]
+    passed[0].start()
+    for d in range(1, groups):
+        copies[d - 1].wait_recv()
+        block = lax.rem(group + groups - d, groups) * 2 + lane
+        copy = pltpu.make_async_remote_copy(
+            src_ref=out_ref.at[block],
+            dst_ref=out_ref.at[block],
+            send_sem=pass_send.at[d],
+            recv_sem=pass_recv.at[d],
+            device_id={axis: sibling},
+            device_id_type=MESH,
+        )
+        copy.start()
+        passed.append(copy)
+    for copy in copies:
+        copy.wait_send()
+    own.wait()
+    for copy in passed:
+        copy.wait()
+
+
+def gather_pairs(x, axis, number):
+    count = lax.axis_size(axis)
+    return pl.pallas_call(
+        functools.partial(gather_pairs_kernel, axis, count // 2),
+        out_shape=jax.ShapeDtypeStruct((count,) + x.shape, x.dtype),
+        in_specs=[pl.BlockSpec(memory_space=pl.ANY)],
+        out_specs=pl.BlockSpec(memory_space=pl.ANY),
+        scratch_shapes=[
+            pltpu.SemaphoreType.DMA,
+            pltpu.SemaphoreType.DMA((count // 2 - 1,)),
+            pltpu.SemaphoreType.DMA((count // 2 - 1,)),
+            pltpu.SemaphoreType.DMA((count // 2,)),
+            pltpu.SemaphoreType.DMA((count // 2,)),
+        ],
+        compiler_params=pltpu.CompilerParams(collective_id=number, has_side_effects=True),
+        cost_estimate=pl.CostEstimate(
+            flops=0, bytes_accessed=2 * count * x.size * x.dtype.itemsize, transcendentals=0
+        ),
+    )(x)
+
+
+def pair_sum(halves, number):
+    lane = lax.rem(lax.axis_index("exp"), 2)
+    both = pair_send(halves, number)
+    own = lax.dynamic_index_in_dim(halves, lane, 0, keepdims=False)
+    return (own.astype(jnp.float32) + both.astype(jnp.float32)).astype(jnp.bfloat16)
+
+
+def pair_kernel(x_ref, out_ref, send_sem, recv_sem):
+    index = lax.axis_index("exp")
+    lane = lax.rem(index, 2)
+    sibling = index + 1 - 2 * lane
+    barrier = pltpu.get_barrier_semaphore()
+    pl.semaphore_signal(barrier, inc=1, device_id={"exp": sibling}, device_id_type=MESH)
+    pl.semaphore_wait(barrier, 1)
+    copy = pltpu.make_async_remote_copy(
+        src_ref=x_ref.at[1 - lane],
+        dst_ref=out_ref,
+        send_sem=send_sem,
+        recv_sem=recv_sem,
+        device_id={"exp": sibling},
+        device_id_type=MESH,
+    )
+    copy.start()
+    copy.wait()
+
+
+def pair_send(halves, number):
+    return pl.pallas_call(
+        pair_kernel,
+        out_shape=jax.ShapeDtypeStruct(halves.shape[1:], halves.dtype),
+        in_specs=[pl.BlockSpec(memory_space=pl.ANY)],
+        out_specs=pl.BlockSpec(memory_space=pl.ANY),
+        scratch_shapes=[pltpu.SemaphoreType.DMA, pltpu.SemaphoreType.DMA],
+        compiler_params=pltpu.CompilerParams(collective_id=number, has_side_effects=True),
+        cost_estimate=pl.CostEstimate(
+            flops=0, bytes_accessed=halves.size * 2, transcendentals=0
+        ),
+    )(halves)
 
 
 def slot_tables(block_ids):
@@ -100,12 +276,23 @@
     device_state = running
     device_decay = decay_run
 
-    def forward(turn_index, incoming):
-        return passed_along(
-            (device_decay[:, None, None] * incoming + device_state).astype(jnp.bfloat16), "ctx", 1
-        ).astype(jnp.float32)
-
-    device_in = lax.fori_loop(0, lax.axis_size("ctx") - 1, forward, jnp.zeros_like(device_state))
+    all_states, all_decays = sent(
+        [
+            device_state.astype(jnp.bfloat16),
+            jnp.broadcast_to(device_decay[:, None], (heads_dev, 128)),
+        ],
+        "ctx",
+        1,
+        True,
+    )
+    ctx_index = lax.axis_index("ctx")
+    device_in = jnp.zeros_like(device_state)
+    for j in range(lax.axis_size("ctx") - 1):
+        device_in = jnp.where(
+            j < ctx_index,
+            all_decays[j, :, :1, None] * device_in + all_states[j].astype(jnp.float32),
+            device_in,
+        )
     entering = jnp.stack(entering_list, axis=1)
     reach = jnp.stack(reach_list, axis=1)
     states = entering + reach[:, :, None, None] * device_in[:, None]
@@ -120,51 +307,59 @@
     grouped = gated_out.reshape(tok_rows, -1, NORM_GROUP)
     group_scale = lax.rsqrt(jnp.mean(grouped * grouped, axis=2, keepdims=True) + EPSILON)
     normed = ((grouped * group_scale).reshape(tok_rows, -1) * norm_gain).astype(jnp.bfloat16)
-    ssm_terms = jnp.dot(
-        normed,
-        lax.all_gather(out_weight, "ctx", axis=1, tiled=True),
-        preferred_element_type=jnp.float32,
-    )
+    ctx_count = lax.axis_size("ctx")
     exp_count = lax.axis_size("exp")
     exp_index = lax.axis_index("exp")
-    slice_width = residual.shape[1] // exp_count
+    width = residual.shape[1]
+    slice_width = width // exp_count
     split_count = exp_count // EXPERTS
-    own_residual = lax.dynamic_slice_in_dim(residual, exp_index * slice_width, slice_width, 1)
-    ssm_sum = lax.psum(ssm_terms.astype(jnp.bfloat16), "exp").astype(jnp.float32)
-    ssm_share = lax.dynamic_slice_in_dim(ssm_sum, exp_index * slice_width, slice_width, 1)
-    stream_slice = (own_residual.astype(jnp.float32) + ssm_share).astype(jnp.bfloat16)
+    own_rows = tok_rows // exp_count
+    normed_all = sent([normed], "ctx", 2, True)[0].reshape(ctx_count * tok_rows, -1)
+    ssm_terms = jnp.dot(normed_all, out_weight, preferred_element_type=jnp.float32).astype(
+        jnp.bfloat16
+    )
+    groups = exp_count // 2
+    by_owner = jnp.transpose(
+        ssm_terms.reshape(ctx_count, groups, 2, own_rows, -1), (2, 1, 0, 3, 4)
+    ).reshape(2, groups * ctx_count * own_rows, -1)
+    halves = pair_sum(by_owner, 3)
+    chips = sent([halves.reshape(groups, ctx_count * own_rows, -1)], "exp", 4, False, 2)[0]
+    ssm_part = jnp.sum(chips.astype(jnp.float32), axis=0).astype(jnp.bfloat16)
+    ssm_rows = sent([ssm_part.reshape(ctx_count, own_rows, -1)], "ctx", 5, False)[0]
+    ssm_rows = jnp.transpose(ssm_rows, (1, 0, 2)).reshape(own_rows, width)
+    own_residual = lax.dynamic_slice_in_dim(residual, exp_index * own_rows, own_rows, 0)
+    stream_rows = (own_residual.astype(jnp.float32) + ssm_rows.astype(jnp.float32)).astype(
+        jnp.bfloat16
+    )
     token_of_slot, pick_rank = slot_tables(expert_ids)
-    stream_full = lax.all_gather(stream_slice, "exp", axis=1, tiled=True)
+    stream_full = gather_pairs(stream_rows, "exp", 6).reshape(tok_rows, width)
+    stream_slice = lax.dynamic_slice_in_dim(stream_full, exp_index * slice_width, slice_width, 1)
     padded = jnp.concatenate(
         [stream_full, jnp.zeros((1, stream_full.shape[1]), jnp.bfloat16)], axis=0
     )
     my_slots = lax.dynamic_index_in_dim(token_of_slot, exp_index // split_count, 0, keepdims=False)
     picked = normalize(jnp.take(padded, my_slots, axis=0), moe_gain)
-    normed_rows = lax.all_gather(picked, "ctx", axis=0, tiled=True)
+    normed_rows = sent([picked], "ctx", 7, True)[0].reshape(ctx_count * CAP, width)
     gate_val = jnp.dot(normed_rows, gate_weight[0], preferred_element_type=jnp.float32)
     up_val = jnp.dot(normed_rows, up_weight[0], preferred_element_type=jnp.float32)
     hidden = (jax.nn.silu(gate_val) * up_val).astype(jnp.bfloat16)
-    sums_mine = lax.psum_scatter(
-        jnp.dot(hidden, down_weight[0], preferred_element_type=jnp.float32).astype(jnp.bfloat16),
-        "ctx",
-        scatter_dimension=0,
-        tiled=True,
-    ).astype(jnp.float32)
-    arrived = lax.all_to_all(
-        sums_mine.astype(jnp.bfloat16), "exp", split_axis=1, concat_axis=0, tiled=True
-    ).astype(sums_mine.dtype)
+    terms = jnp.dot(hidden, down_weight[0], preferred_element_type=jnp.float32).astype(
+        jnp.bfloat16
+    )
+    arrived_terms = sent([terms.reshape(ctx_count, CAP, width)], "ctx", 8, False)[0]
+    sums_mine = jnp.sum(arrived_terms.astype(jnp.float32), axis=0).astype(jnp.bfloat16)
+    arrived = lax.all_to_all(sums_mine, "exp", split_axis=1, concat_axis=0, tiled=True)
     piece_expert = jnp.arange(exp_count, dtype=jnp.int32) // split_count
-    hit_expert = (expert_ids[:, :, None] == piece_expert[None, None, :]).astype(jnp.float32)
-    hit_slot = (pick_rank[:, :, None] == jnp.arange(CAP, dtype=jnp.int32)[None, None, :]).astype(
-        jnp.float32
-    )
-    combine_table = jnp.sum(
-        route_weight[:, :, None, None] * hit_expert[:, :, :, None] * hit_slot[:, :, None, :], axis=1
-    )
-    combine_table = combine_table.reshape(tok_rows, exp_count * CAP)
-    moe_slice = jnp.dot(
-        combine_table, arrived, precision=lax.Precision.HIGHEST, preferred_element_type=jnp.float32
-    )
+    slot_range = jnp.arange(CAP, dtype=jnp.int32)
+    moe_slice = jnp.zeros((tok_rows, slice_width), jnp.float32)
+    for k in range(expert_ids.shape[1]):
+        hit_expert = expert_ids[:, k, None] == piece_expert[None, :]
+        hit_slot = pick_rank[:, k, None] == slot_range[None, :]
+        hits = (hit_expert[:, :, None] & hit_slot[:, None, :]).astype(jnp.bfloat16)
+        picked_out = jnp.dot(
+            hits.reshape(tok_rows, exp_count * CAP), arrived, preferred_element_type=jnp.float32
+        )
+        moe_slice = moe_slice + route_weight[:, k, None] * picked_out
     return (stream_slice.astype(jnp.float32) + moe_slice).astype(jnp.bfloat16)
 
 

time: 344 us -> 225 us (0.65)
  waiting for transfers between devices: 246 us -> 12.8 us
  Pallas kernels: 0 us -> 122 us
  other arithmetic: 5.34 us -> 19.5 us
  starting transfers between devices: 18.6 us -> 5.2 us
  between operations: 13.5 us -> 0.41 us
    pallas_call x0 -> x8, Pallas kernels: none -> 122 us  [the longest x6 104 us: sent(): pl.pallas_call(functools.partial(send_kernel, axis, count, pair, spread,...]
    all_gather x3 -> x0, waiting for transfers between devices: 109 us -> none  [the longest x1 54.2 us: body(): lax.all_gather(out_weight, 'ctx', axis=1, tiled=True)]
    psum x1 -> x0, waiting for transfers between devices: 58.9 us -> none  [body(): lax.psum(ssm_terms.astype(jnp.bfloat16), 'exp').astype(jnp.float32)]
    reduce_scatter x1 -> x0, waiting for transfers between devices: 35.4 us -> none  [body(): lax.psum_scatter(jnp.dot(hidden, down_weight[0], preferred_element_type=j...]
    ppermute x3 -> x0, waiting for transfers between devices: 28.4 us -> none  [passed_along(): return lax.ppermute(block, axis, route)]
    ppermute x3 -> x0, starting transfers between devices: 13.7 us -> none  [passed_along(): return lax.ppermute(block, axis, route)]
    reduce_sum x1 -> x2, other arithmetic: 0.04 us -> 3.79 us  [the longest x1 1.98 us: body(): jnp.sum(arrived_terms.astype(jnp.float32), axis=0).astype(jnp.bfloat16)]
    dot_general x2 -> x3, matrix products: 6.91 us -> 4.61 us  [the longest x1 2.48 us: body(): jnp.dot(normed_all, out_weight, preferred_element_type=jnp.float32)]
  transfers between devices with their start and end apart: 9 -> 1, of which waited for: 9 -> 1; matrix products, arithmetic and copies ran while one was open for 3% -> 1% of each run, Pallas kernels for 0% -> 0%
where the time goes in v1:
time: 225 us; the launch traced here: 224 us
  Pallas kernels  122 us (54%)
  matrix products  52 us (23%)
  other arithmetic  19.5 us (9%)
  waiting for transfers between devices  12.8 us (6%)
  local copies, waits for them, and re-layouts  12 us (5%)
  starting transfers between devices  5.2 us (2%)
    pallas_call x6, Pallas kernels, sent(): pl.pallas_call(functools.partial(send_kernel, axis, count, pair, spread,...  104 us
    dot_general x1, matrix products, body(): jnp.dot(hidden, down_weight[0], preferred_element_type=jnp.float32)  25.1 us
    dot_general x1, matrix products, body(): jnp.dot(normed_rows, gate_weight[0], preferred_element_type=jnp.float32)  16.9 us
    pallas_call x1, Pallas kernels, gather_pairs(): pl.pallas_call(functools.partial(gather_pairs_kernel, axis, count // 2),...  16.3 us
    all_to_all x1, waiting for transfers between devices, body(): lax.all_to_all(sums_mine, 'exp', split_axis=1, concat_axis=0, tiled=True)  12.8 us
    all_to_all x1, starting transfers between devices, body(): lax.all_to_all(sums_mine, 'exp', split_axis=1, concat_axis=0, tiled=True)  5.2 us
  transfers between devices with their start and end apart: 1, of which 1 were waited for; matrix products, arithmetic and copies ran while one was open for 1% of the time, Pallas kernels for 0%

profile of v1, /device:TPU:0, one launch (start us, length us, event | category | flops | bytes accessed | tf_op | source)
XLA Modules:
  0.0 224.1 jit_solution(16788364902208183594)
XLA Ops:
  5.5 1.1 copy.78
  6.6 1.2 copy.79
  8.6 0.9 fusion.89
  10.1 1.2 fusion.32.refs_0_
  12.0 16.9 %shard_map.154 = (bf16[4,16,64,128]{3,2,1,0:T(8,128)(2,1)}, f32[4,16,128]{2,1,0:T(8,128)}) custom-call(bf16[16,64,128]{2,1,0:T(8,128)(2,1)} %fusion.32.refs_0_, f32[16,128]{1,0:T(8,128)} %broadcast_in_dim.46.refs_1_), custom_call_target="tpu_custom_call" | custom-call | bytes 2162688 | tf_op jit(solution)/shard_map/pallas_call | solution.py:67
  29.9 1.7 fusion.24
  31.6 1.5 fusion.26
  33.3 0.9 fusion.88
  34.3 1.5 mul.245
  37.2 15.1 %shard_map.155 = bf16[4,128,1024]{2,1,0:T(8,128)(2,1)} custom-call(bf16[128,1024]{1,0:T(8,128)(2,1)} %multiply_convert_fusion.2.refs_0_), custom_call_target="tpu_custom_call" | custom-call | bytes 2097152 | tf_op jit(solution)/shard_map/pallas_call | solution.py:67
  52.4 2.5 %convolution_convert_fusion = bf16[512,1024]{1,0:T(8,128)(2,1)S(1)} fusion(bf16[512,1024]{1,0:T(8,128)(2,1)} %bitcast.141, bf16[1024,1024]{1,0:T(8,128)(2,1)S(1)} %copy-done), kind=kOutput, calls=%fused_computation.17 | convolution fusion | flops 1074266112 | bytes 4194304 | tf_op jit(solution)/shard_map/dot_general | solution.py:318
  54.9 1.1 copy.83
  56.0 2.3 %shard_map.156 = bf16[256,1024]{1,0:T(8,128)(2,1)} custom-call(bf16[2,256,1024]{2,1,0:T(8,128)(2,1)} %bitcast.130), custom_call_target="tpu_custom_call" | custom-call | bytes 1048576 | tf_op jit(solution)/shard_map/pallas_call | solution.py:184
  58.3 2.2 fusion.37
  60.5 13.7 %shard_map.157 = bf16[4,64,1024]{2,1,0:T(8,128)(2,1)} custom-call(bf16[4,64,1024]{2,1,0:T(8,128)(2,1)} %bitcast.138), custom_call_target="tpu_custom_call" | custom-call | bytes 1048576 | tf_op jit(solution)/shard_map/pallas_call | solution.py:67
  74.2 1.8 reduce_sum.61
  76.0 5.2 %shard_map.158 = bf16[4,16,1024]{2,1,0:T(8,128)(2,1)} custom-call(bf16[4,16,1024]{2,1,0:T(8,128)(2,1)} %bitcast.146), custom_call_target="tpu_custom_call" | custom-call | bytes 262144 | tf_op jit(solution)/shard_map/pallas_call | solution.py:67
  81.2 0.9 convert_bitcast_fusion
  82.1 1.6 add_convert_fusion.x_ref
  83.7 16.3 %shard_map.159 = bf16[8,16,4096]{2,1,0:T(8,128)(2,1)} custom-call(bf16[16,4096]{1,0:T(8,128)(2,1)} %add_convert_fusion.x_ref), custom_call_target="tpu_custom_call" | custom-call | bytes 2097152 | tf_op jit(solution)/shard_map/pallas_call | solution.py:138
  100.0 1.3 concatenate.3
  101.4 1.1 gather_fusion
  102.9 1.0 fusion.36.refs_0_
  103.9 26.2 %shard_map.160 = bf16[4,64,4096]{2,1,0:T(8,128)(2,1)} custom-call(bf16[64,4096]{1,0:T(8,128)(2,1)} %fusion.36.refs_0_), custom_call_target="tpu_custom_call" | custom-call | bytes 4194304 | tf_op jit(solution)/shard_map/pallas_call | solution.py:67
  130.1 16.9 %fusion.4 = f32[256,3072]{1,0:T(8,128)} fusion(bf16[256,4096]{1,0:T(8,128)(2,1)} %bitcast.134, bf16[1,4096,3072]{2,1,0:T(8,128)(2,1)} %param.27), kind=kOutput, calls=%fused_computation.6 | convolution fusion | flops 6442450944 | bytes 30408704 | tf_op jit(solution)/shard_map/dot_general | solution.py:343
  147.0 25.1 %fusion.6 = bf16[256,4096]{1,0:T(8,128)(2,1)} fusion(bf16[1,3072,4096]{2,1,0:T(8,128)(2,1)} %param.29, bf16[256,4096]{1,0:T(8,128)(2,1)S(1)} %bitcast.135, bf16[1,4096,3072]{2,1,0:T(8,128)(2,1)} %param.28, f32[256,3072]{1,0:T(8,128)} %fusion.4), kind=kOutput, calls=%fused_computation.8 | convolution fusion | flops 12890669056 | bytes 57671680 | tf_op jit(solution)/shard_map/dot_general | solution.py:346
  172.1 26.4 %shard_map.161 = bf16[4,64,4096]{2,1,0:T(8,128)(2,1)} custom-call(bf16[4,64,4096]{2,1,0:T(8,128)(2,1)} %bitcast.137), custom_call_target="tpu_custom_call" | custom-call | bytes 4194304 | tf_op jit(solution)/shard_map/pallas_call | solution.py:67
  198.5 2.0 reduce_sum.65
  201.3 5.2 %all-to-all-start = ((bf16[64,8,512]{2,0,1:T(8,128)(2,1)}), bf16[64,8,512]{2,0,1:T(8,128)(2,1)S(1)}, u32[]{:S(2)}, u32[]{:S(2)}) async-start(bf16[64,8,512]{2,0,1:T(8,128)(2,1)} %bitcast.129), calls=%async_computation | async-start | bytes 1048576 | tf_op jit(solution)/shard_map/all_to_all | solution.py:351
  206.9 1.9 gather_fusion.1
  209.1 12.8 %all-to-all-done = bf16[64,8,512]{2,0,1:T(8,128)(2,1)S(1)} async-done(((bf16[64,8,512]{2,0,1:T(8,128)(2,1)}), bf16[64,8,512]{2,0,1:T(8,128)(2,1)S(1)}, u32[]{:S(2)}, u32[]{:S(2)}) %all-to-all-start) | async-done | bytes 524320 | tf_op jit(solution)/shard_map/all_to_all | solution.py:351
  222.2 1.9 fusion.33
  (67 shorter events, 12.0 us)
Async XLA Ops:
  0.0 52.4 %copy-start = (bf16[1024,1024]{1,0:T(8,128)(2,1)S(1)}, bf16[1024,1024]{1,0:T(8,128)(2,1)}, u32[]{:S(2)}) copy-start(bf16[1024,1024]{1,0:T(8,128)(2,1)} %param.25) | copy-start | bytes 6291460
  0.0 29.8 %copy-start.5 = (bf16[128,128]{1,0:T(8,128)(2,1)S(1)}, bf16[128,128]{1,0:T(8,128)(2,1)}, u32[]{:S(2)}) copy-start(bf16[128,128]{1,0:T(8,128)(2,1)} %param.20) | copy-start | bytes 98308
  6.6 3.5 %copy-start.4 = (bf16[128,1024]{0,1:T(8,128)(2,1)}, bf16[128,1024]{0,1:T(8,128)(2,1)S(1)}, u32[]{:S(2)}) copy-start(bf16[128,1024]{0,1:T(8,128)(2,1)S(1)} %copy.78) | copy-start | bytes 786436
  11.4 22.0 %copy-start.3 = (bf16[128,1024]{1,0:T(8,128)(2,1)S(1)}, bf16[128,1024]{1,0:T(8,128)(2,1)}, u32[]{:S(2)}) copy-start(bf16[128,1024]{1,0:T(8,128)(2,1)} %param.18) | copy-start | bytes 786436
  33.1 3.2 %copy-start.8 = (f32[1024]{0:T(1024)S(1)}, f32[1024]{0:T(1024)}, u32[]{:S(2)}) copy-start(f32[1024]{0:T(1024)} %param.24) | copy-start | bytes 12292
  100.0 2.5 %copy-start.9 = (pred[64]{0:T(512)(128)(4,1)S(1)}, pred[64]{0:T(512)(128)(4,1)}, u32[]{:S(2)}) copy-start(pred[64]{0:T(512)(128)(4,1)} %compare_and_fusion) | copy-start | bytes 196
  101.4 1.5 copy-start.6
  130.1 16.9 %copy-start.2 = (bf16[4,64,4096]{2,1,0:T(8,128)(2,1)S(1)}, bf16[4,64,4096]{2,1,0:T(8,128)(2,1)}, u32[]{:S(2)}) copy-start(bf16[4,64,4096]{2,1,0:T(8,128)(2,1)} %shard_map.160) | copy-start | bytes 6291460
  198.5 8.1 %copy-start.7 = (s32[128,2]{0,1:T(2,128)S(1)}, s32[128,2]{0,1:T(2,128)}, u32[]{:S(2)}) copy-start(s32[128,2]{0,1:T(2,128)} %param.30) | copy-start | bytes 3076
  198.5 8.1 %copy-start.10 = (f32[128,2]{0,1:T(2,128)S(1)}, f32[128,2]{0,1:T(2,128)}, u32[]{:S(2)}) copy-start(f32[128,2]{0,1:T(2,128)} %param.31) | copy-start | bytes 3076
  201.3 20.6 %all-to-all-start = ((bf16[64,8,512]{2,0,1:T(8,128)(2,1)}), bf16[64,8,512]{2,0,1:T(8,128)(2,1)S(1)}, u32[]{:S(2)}, u32[]{:S(2)}) async-start(bf16[64,8,512]{2,0,1:T(8,128)(2,1)} %bitcast.129), calls=%async_computation | async-start | bytes 1048576 | tf_op jit(solution)/shard_map/all_to_all | solution.py:351
  206.9 17.2 %copy-start.1 = (bf16[1024,1024]{1,0:T(8,128)(2,1)S(1)}, bf16[1024,1024]{1,0:T(8,128)(2,1)}, u32[]{:S(2)}) copy-start(bf16[1024,1024]{1,0:T(8,128)(2,1)} %param.25) | copy-start | bytes 6291460

commit v2 on v1

--- a/solution.py
+++ b/solution.py
@@ -192,6 +192,53 @@
             flops=0, bytes_accessed=halves.size * 2, transcendentals=0
         ),
     )(halves)
+
+
+def expert_kernel(x_ref, gate_ref, up_ref, down_ref, out_ref, total):
+    step = pl.program_id(1)
+    gate_val = jnp.dot(x_ref[...], gate_ref[...], preferred_element_type=jnp.float32)
+    up_val = jnp.dot(x_ref[...], up_ref[...], preferred_element_type=jnp.float32)
+    hidden = (gate_val / (1.0 + jnp.exp(-gate_val)) * up_val).astype(jnp.bfloat16)
+    columns = down_ref.shape[1] // 4
+
+    def add(first):
+        for c in range(4):
+            part = slice(c * columns, (c + 1) * columns)
+            term = jnp.dot(hidden, down_ref[:, part], preferred_element_type=jnp.float32)
+            total[:, part] = term if first else total[:, part] + term
+
+    pl.when(step == 0)(lambda: add(True))
+    pl.when(step > 0)(lambda: add(False))
+
+    @pl.when(step == pl.num_programs(1) - 1)
+    def _():
+        out_ref[...] = total[...].astype(out_ref.dtype)
+
+
+def expert_terms(rows, gate, up, down):
+    count, width = rows.shape
+    units = gate.shape[1]
+    block = 256 if units % 256 == 0 else 128
+    tall = 256 if count % 256 == 0 else count
+    return pl.pallas_call(
+        expert_kernel,
+        out_shape=jax.ShapeDtypeStruct((count, width), jnp.bfloat16),
+        grid=(count // tall, units // block),
+        in_specs=[
+            pl.BlockSpec((tall, width), lambda r, i: (r, 0)),
+            pl.BlockSpec((width, block), lambda r, i: (0, i)),
+            pl.BlockSpec((width, block), lambda r, i: (0, i)),
+            pl.BlockSpec((block, width), lambda r, i: (i, 0)),
+        ],
+        out_specs=pl.BlockSpec((tall, width), lambda r, i: (r, 0)),
+        scratch_shapes=[pltpu.VMEM((tall, width), jnp.float32)],
+        compiler_params=pltpu.CompilerParams(vmem_limit_bytes=48 * 1024 * 1024),
+        cost_estimate=pl.CostEstimate(
+            flops=6 * count * width * units,
+            bytes_accessed=6 * width * units,
+            transcendentals=count * units,
+        ),
+    )(rows, gate, up, down)
 
 
 def slot_tables(block_ids):
@@ -340,15 +387,11 @@
     my_slots = lax.dynamic_index_in_dim(token_of_slot, exp_index // split_count, 0, keepdims=False)
     picked = normalize(jnp.take(padded, my_slots, axis=0), moe_gain)
     normed_rows = sent([picked], "ctx", 7, True)[0].reshape(ctx_count * CAP, width)
-    gate_val = jnp.dot(normed_rows, gate_weight[0], preferred_element_type=jnp.float32)
-    up_val = jnp.dot(normed_rows, up_weight[0], preferred_element_type=jnp.float32)
-    hidden = (jax.nn.silu(gate_val) * up_val).astype(jnp.bfloat16)
-    terms = jnp.dot(hidden, down_weight[0], preferred_element_type=jnp.float32).astype(
-        jnp.bfloat16
-    )
+    terms = expert_terms(normed_rows, gate_weight[0], up_weight[0], down_weight[0])
     arrived_terms = sent([terms.reshape(ctx_count, CAP, width)], "ctx", 8, False)[0]
     sums_mine = jnp.sum(arrived_terms.astype(jnp.float32), axis=0).astype(jnp.bfloat16)
-    arrived = lax.all_to_all(sums_mine, "exp", split_axis=1, concat_axis=0, tiled=True)
+    by_slice = jnp.transpose(sums_mine.reshape(CAP, exp_count, slice_width), (1, 0, 2))
+    arrived = sent([by_slice], "exp", 9, False)[0].reshape(exp_count * CAP, slice_width)
     piece_expert = jnp.arange(exp_count, dtype=jnp.int32) // split_count
     slot_range = jnp.arange(CAP, dtype=jnp.int32)
     moe_slice = jnp.zeros((tok_rows, slice_width), jnp.float32)

time: 225 us -> 216 us (0.960)
  Pallas kernels: 122 us -> 168 us
  matrix products: 52 us -> 11 us
  waiting for transfers between devices: 12.8 us -> 0 us
  starting transfers between devices: 5.2 us -> 0 us
  local copies, waits for them, and re-layouts: 12 us -> 15.9 us
    dot_general x2 -> x0, matrix products: 42 us -> none  [the longest x1 25.1 us: body(): jnp.dot(hidden, down_weight[0], preferred_element_type=jnp.float32)]
    pallas_call x0 -> x1, Pallas kernels: none -> 32.1 us  [expert_terms(): pl.pallas_call(expert_kernel, out_shape=jax.ShapeDtypeStruct((count, widt...]
    pallas_call x6 -> x7, Pallas kernels: 104 us -> 117 us  [sent(): pl.pallas_call(functools.partial(send_kernel, axis, count, pair, spread,...]
    all_to_all x1 -> x0, waiting for transfers between devices: 12.8 us -> none  [body(): lax.all_to_all(sums_mine, 'exp', split_axis=1, concat_axis=0, tiled=True)]
    all_to_all x1 -> x0, starting transfers between devices: 5.2 us -> none  [body(): lax.all_to_all(sums_mine, 'exp', split_axis=1, concat_axis=0, tiled=True)]
    unnamed x24 -> x28, local copies, waits for them, and re-layouts: 1.27 us -> 3.97 us
  transfers between devices with their start and end apart: 1 -> 0, of which waited for: 1 -> 0; matrix products, arithmetic and copies ran while one was open for 1% -> 0% of each run, Pallas kernels for 0% -> 0%
where the time goes in v2:
time: 216 us; the launch traced here: 214 us
  Pallas kernels  168 us (78%)
  other arithmetic  18.7 us (9%)
  local copies, waits for them, and re-layouts  15.9 us (7%)
  matrix products  11 us (5%)
    pallas_call x7, Pallas kernels, sent(): pl.pallas_call(functools.partial(send_kernel, axis, count, pair, spread,...  117 us
    pallas_call x1, Pallas kernels, expert_terms(): pl.pallas_call(expert_kernel, out_shape=jax.ShapeDtypeStruct((count, widt...  32.1 us
    pallas_call x1, Pallas kernels, gather_pairs(): pl.pallas_call(functools.partial(gather_pairs_kernel, axis, count // 2),...  16.3 us

profile of v2, /device:TPU:0, one launch (start us, length us, event | category | flops | bytes accessed | tf_op | source)
XLA Modules:
  0.0 213.8 jit_solution(7214286192002514586)
XLA Ops:
  7.7 0.9 fusion.63
  8.7 1.9 gather_fusion.1
  12.4 1.2 fusion.9.refs_0_
  13.8 17.0 %shard_map.154 = (bf16[4,16,64,128]{3,2,1,0:T(8,128)(2,1)}, f32[4,16,128]{2,1,0:T(8,128)}) custom-call(bf16[16,64,128]{2,1,0:T(8,128)(2,1)} %fusion.9.refs_0_, f32[16,128]{1,0:T(8,128)} %broadcast_in_dim.46.refs_1_), custom_call_target="tpu_custom_call" | custom-call | bytes 2162688 | tf_op jit(solution)/shard_map/pallas_call | solution.py:67
  31.7 1.7 fusion.1
  33.5 1.4 fusion.3
  34.8 1.2 copy.80
  36.1 0.9 fusion.62
  37.1 1.5 mul.238
  39.1 0.9 multiply_convert_fusion.2.refs_0_
  40.0 15.1 %shard_map.155 = bf16[4,128,1024]{2,1,0:T(8,128)(2,1)} custom-call(bf16[128,1024]{1,0:T(8,128)(2,1)} %multiply_convert_fusion.2.refs_0_), custom_call_target="tpu_custom_call" | custom-call | bytes 2097152 | tf_op jit(solution)/shard_map/pallas_call | solution.py:67
  55.2 2.5 %convolution_convert_fusion = bf16[512,1024]{1,0:T(8,128)(2,1)S(1)} fusion(bf16[512,1024]{1,0:T(8,128)(2,1)} %bitcast.128, bf16[1024,1024]{1,0:T(8,128)(2,1)S(1)} %copy-done), kind=kOutput, calls=%fused_computation.2 | convolution fusion | flops 1074266112 | bytes 4194304 | tf_op jit(solution)/shard_map/dot_general | solution.py:365
  57.6 1.1 copy.83
  58.7 2.3 %shard_map.156 = bf16[256,1024]{1,0:T(8,128)(2,1)} custom-call(bf16[2,256,1024]{2,1,0:T(8,128)(2,1)} %bitcast.119), custom_call_target="tpu_custom_call" | custom-call | bytes 1048576 | tf_op jit(solution)/shard_map/pallas_call | solution.py:184
  61.0 2.2 %fusion.14 = bf16[256,1024]{1,0:T(8,128)(2,1)} fusion(bf16[256,1024]{1,0:T(8,128)(2,1)} %shard_map.156, bf16[2,256,1024]{2,1,0:T(8,128)(2,1)} %bitcast.120, s32[]{:T(128)S(6)} %select_n.116), kind=kLoop, calls=%fused_computation.25 | loop fusion | flops 1048576 | bytes 1572868 | tf_op jit(solution)/shard_map/convert_element_type | solution.py:161
  63.2 13.7 %shard_map.157 = bf16[4,64,1024]{2,1,0:T(8,128)(2,1)} custom-call(bf16[4,64,1024]{2,1,0:T(8,128)(2,1)} %bitcast.124), custom_call_target="tpu_custom_call" | custom-call | bytes 1048576 | tf_op jit(solution)/shard_map/pallas_call | solution.py:67
  76.9 1.8 reduce_sum.61
  78.8 5.2 %shard_map.158 = bf16[4,16,1024]{2,1,0:T(8,128)(2,1)} custom-call(bf16[4,16,1024]{2,1,0:T(8,128)(2,1)} %bitcast.133), custom_call_target="tpu_custom_call" | custom-call | bytes 262144 | tf_op jit(solution)/shard_map/pallas_call | solution.py:67
  84.0 0.9 convert_bitcast_fusion
  84.9 1.6 add_convert_fusion.x_ref
  86.5 16.3 %shard_map.159 = bf16[8,16,4096]{2,1,0:T(8,128)(2,1)} custom-call(bf16[16,4096]{1,0:T(8,128)(2,1)} %add_convert_fusion.x_ref), custom_call_target="tpu_custom_call" | custom-call | bytes 2097152 | tf_op jit(solution)/shard_map/pallas_call | solution.py:138
  102.8 1.3 concatenate.3
  105.4 1.0 fusion.13.refs_0_
  106.4 26.2 %shard_map.160 = bf16[4,64,4096]{2,1,0:T(8,128)(2,1)} custom-call(bf16[64,4096]{1,0:T(8,128)(2,1)} %fusion.13.refs_0_), custom_call_target="tpu_custom_call" | custom-call | bytes 4194304 | tf_op jit(solution)/shard_map/pallas_call | solution.py:67
  132.6 1.6 copy-done.2
  134.2 32.1 %shard_map.161 = bf16[256,4096]{1,0:T(8,128)(2,1)S(1)} custom-call(bf16[256,4096]{1,0:T(8,128)(2,1)S(1)} %bitcast.114, bf16[4096,3072]{1,0:T(8,128)(2,1)} %bitcast.116, bf16[4096,3072]{1,0:T(8,128)(2,1)} %bitcast.117, bf16[3072,4096]{1,0:T(8,128)(2,1)} %bitcast.118), custom_call_target="tpu_custom_call" | custom-call | flops 19327352832 | bytes 75497472 | tf_op jit(solution)/shard_map/pallas_call | solution.py:223
  166.3 1.3 copy-done.3
  167.7 26.4 %shard_map.162 = bf16[4,64,4096]{2,1,0:T(8,128)(2,1)} custom-call(bf16[4,64,4096]{2,1,0:T(8,128)(2,1)} %bitcast.115), custom_call_target="tpu_custom_call" | custom-call | bytes 4194304 | tf_op jit(solution)/shard_map/pallas_call | solution.py:67
  194.1 2.1 reduce_sum.65
  197.1 13.4 %shard_map.163 = bf16[8,64,512]{2,1,0:T(8,128)(2,1)} custom-call(bf16[8,64,512]{2,1,0:T(8,128)(2,1)} %bitcast.126), custom_call_target="tpu_custom_call" | custom-call | bytes 1048576 | tf_op jit(solution)/shard_map/pallas_call | solution.py:67
  210.5 1.3 fusion.7
  211.8 2.0 fusion.10
  (69 shorter events, 13.1 us)
Async XLA Ops:
  0.0 55.1 %copy-start = (bf16[1024,1024]{1,0:T(8,128)(2,1)S(1)}, bf16[1024,1024]{1,0:T(8,128)(2,1)}, u32[]{:S(2)}) copy-start(bf16[1024,1024]{1,0:T(8,128)(2,1)} %param.25) | copy-start | bytes 6291460
  8.7 2.8 %copy-start.10 = (s32[128,2]{0,1:T(2,128)S(1)}, s32[128,2]{0,1:T(2,128)}, u32[]{:S(2)}) copy-start(s32[128,2]{0,1:T(2,128)} %param.30) | copy-start | bytes 3076
  8.7 2.8 %copy-start.4 = (bf16[128,1024]{1,0:T(8,128)(2,1)S(1)}, bf16[128,1024]{1,0:T(8,128)(2,1)}, u32[]{:S(2)}) copy-start(bf16[128,1024]{1,0:T(8,128)(2,1)} %param.17) | copy-start | bytes 786436
  10.7 21.0 %copy-start.8 = (bf16[128,128]{1,0:T(8,128)(2,1)S(1)}, bf16[128,128]{1,0:T(8,128)(2,1)}, u32[]{:S(2)}) copy-start(bf16[128,128]{1,0:T(8,128)(2,1)} %param.20) | copy-start | bytes 98308
  11.5 21.9 %copy-start.12 = (f32[16]{0:T(128)S(1)}, f32[16]{0:T(128)}, u32[]{:S(2)}) copy-start(f32[16]{0:T(128)} %param.23) | copy-start | bytes 196
  11.7 0.7 copy-start.6
  13.8 19.6 %copy-start.7 = (bf16[128,1024]{0,1:T(8,128)(2,1)S(1)}, bf16[128,1024]{0,1:T(8,128)(2,1)}, u32[]{:S(2)}) copy-start(bf16[128,1024]{0,1:T(8,128)(2,1)} %copy-done.6) | copy-start | bytes 786436
  33.5 2.6 %copy-start.5 = (bf16[128,1024]{1,0:T(8,128)(2,1)S(1)}, bf16[128,1024]{1,0:T(8,128)(2,1)}, u32[]{:S(2)}) copy-start(bf16[128,1024]{1,0:T(8,128)(2,1)} %param.18) | copy-start | bytes 786436
  36.1 3.0 %copy-start.11 = (f32[1024]{0:T(1024)S(1)}, f32[1024]{0:T(1024)}, u32[]{:S(2)}) copy-start(f32[1024]{0:T(1024)} %param.24) | copy-start | bytes 12292
  104.1 1.2 copy-start.9
  132.6 1.6 copy-start.2
  166.3 1.4 copy-start.3
  194.1 19.7 %copy-start.1 = (bf16[1024,1024]{1,0:T(8,128)(2,1)S(1)}, bf16[1024,1024]{1,0:T(8,128)(2,1)}, u32[]{:S(2)}) copy-start(bf16[1024,1024]{1,0:T(8,128)(2,1)} %param.25) | copy-start | bytes 6291460
